TPU v7x, 128 devices: a whole 4x4x4 slice. The times are simulated.
128 devices in a mesh: row: 16 (over x, z_hi, core), col: 8 (over y, z_lo).
Axes of the slice: x: 4, y: 4, z: 4 (z_hi: 2, z_lo: 2; z = z_hi * 2 + z_lo), core: 2. Of those that a mesh axis runs over, the one named last changes fastest.
Arguments:
- tile_values: bfloat16 [256, 8, 4, 128, 128], P(('row', 'col')), may hold values from 0 to 1
- tile_columns: int32 [256, 8, 4], P(('row', 'col')), may hold values from -1 to 255, as said below
- owner_map: int32 [256], replicated, may hold values from 0 to 255, as said below
- section_rows: int32 [2], replicated, may hold values from 0 to 15, as said below
Outputs:
- inflated: bfloat16 [32768, 12288], P('row', 'col')
Inputs may be any that keep to these rules, and one draw needn't show every extreme that they name: `tile_columns`: in each tile row and block-column b, the first 1 to 4 slots name distinct tile columns within b * 32 to b * 32 + 31 and the remaining slots hold -1; some tile row uses all 4 slots. A permutation of the tile rows; of the tile rows t in each aligned group of 16, exactly 1 have owner_map[t] in each block-row's range of 16 positions. `section_rows`: distinct block-rows; the last block-row is always one of them.
All inputs are finite; a program needn't handle non-finite values.
Results may differ from a plain program's by a relative error of at most 0.001.
Values may be sent and summed in bfloat16 or wider, within the bound.
A program may use at most 128 MiB of HBM per device.

v0:
```python
import jax
import jax.numpy as jnp
from jax import lax
from jax.sharding import Mesh
from jax.sharding import PartitionSpec as P

TILE = 128
SLAB = 12
SECTIONS = 2
ROW = ("row_0", "row_1", "row_2")
ROW_COL = ("row_0", "row_1", "row_2", "col")


def cut_along(x, dim, peers):
    dims = x.shape
    tiles = x.reshape(*dims[:dim], peers, dims[dim] // peers, *dims[dim + 1 :])
    return jnp.moveaxis(tiles, dim, 0)


def joined_along(tiles, dim):
    dims = list(tiles.shape[1:])
    dims[dim] *= tiles.shape[0]
    return jnp.moveaxis(tiles, 0, dim).reshape(dims)


def moved_by_axis(tiles, axes, turns):
    inside = tiles.shape[1:]
    out = tiles.reshape(*(lax.axis_size(a) for a in axes), *inside)
    for k in turns:
        out = lax.all_to_all(out, axes[k], k, k, tiled=True)
    return out.reshape(-1, *inside)


def two_step_exchange(x, groups, turns, split_dim, concat_dim):
    peers = lax.axis_size(groups[0]) * lax.axis_size(groups[1])
    tiles = cut_along(x, split_dim, peers)
    return joined_along(moved_by_axis(tiles, groups, turns), concat_dim)


def broadcast(x, axis, root):
    mine = lax.axis_index(axis) == root
    return lax.psum(jnp.where(mine, x, jnp.zeros_like(x)), axis)


def copy_for_each(x, axis):
    peers = lax.axis_size(axis)
    return lax.all_to_all(jnp.broadcast_to(x[None], (peers, *x.shape)), axis, 0, 0, tiled=True)


def over_copies(x, axis):
    return copy_for_each(x, axis).sum(axis=0)


def densify(values_in, columns_in, first_col):
    relative = columns_in - first_col
    picker = (relative[..., None] == jnp.arange(SLAB, dtype=jnp.int32)).astype(jnp.bfloat16)
    spread = jnp.einsum("nkab,nkj->najb", values_in, picker, preferred_element_type=jnp.float32)
    return spread.astype(jnp.bfloat16).reshape(values_in.shape[0], TILE, SLAB * TILE)


def per_device(tile_values, tile_columns, owner_map, section_rows):
    n_row = lax.axis_size(ROW)
    n_col = lax.axis_size("col")
    row_id = lax.axis_index(ROW)
    col_id = lax.axis_index("col")
    tile_count = owner_map.shape[0]
    rows_block = tile_values.shape[0] * n_col
    cols_block = tile_values.shape[0] * n_row
    first_col = col_id * cols_block
    every_columns = lax.all_gather(tile_columns, ROW_COL, axis=0, tiled=True)
    every_tile = jnp.arange(tile_count, dtype=jnp.int32)
    inverse = jnp.zeros((tile_count,), jnp.int32).at[owner_map].set(every_tile)
    grid_columns = every_columns[inverse]

    def block_lists(block_row, block_col):
        rows_part = lax.dynamic_slice_in_dim(grid_columns, block_row * rows_block, rows_block, 0)
        return jnp.take(rows_part, block_col, axis=1)

    spread_vals = lax.all_to_all(tile_values, "col", split_axis=1, concat_axis=0, tiled=True)
    spread_vals = spread_vals[:, 0]
    local_rows = jnp.arange(rows_block, dtype=jnp.int32)
    source_tiles = row_id * rows_block + local_rows
    target_block = owner_map[source_tiles] // rows_block
    send_order = jnp.argsort(target_block * rows_block + local_rows)
    recv_vals = two_step_exchange(
        spread_vals[send_order], (("row_0", "row_1"), "row_2"), (1, 0), 0, 0
    )
    owned = owner_map // rows_block == row_id
    arrived = jnp.argsort(jnp.where(owned, every_tile, every_tile + tile_count))[:rows_block]
    new_local = owner_map[arrived] - row_id * rows_block
    placed = jnp.argsort(new_local)
    block_vals = recv_vals[placed]
    slot_values = []
    slot_targets = []
    panels = []
    for section in range(SECTIONS):
        section_row = section_rows[section]
        source_col = section_row * n_col // n_row
        panel_vals = broadcast(block_vals, "col", source_col)
        panel_cols = block_lists(row_id, source_col)
        list_vals = broadcast(block_vals, ROW, section_row)
        panel_dense = densify(list_vals, block_lists(section_row, col_id), first_col)
        relative = panel_cols - section_row * rows_block
        inside = (relative >= 0) & (relative < rows_block)
        slot_targets.append(jnp.where(inside, relative, 0) + section * rows_block)
        slot_values.append(panel_vals * inside[..., None, None].astype(jnp.bfloat16))
        panels.append(panel_dense)
    all_values = jnp.concatenate(slot_values, axis=1)
    all_targets = jnp.concatenate(slot_targets, axis=1)
    all_panels = jnp.concatenate(panels, axis=0).reshape(SECTIONS * rows_block * TILE, SLAB * TILE)
    inner_count = SECTIONS * rows_block
    left_picker = (all_targets[..., None] == jnp.arange(inner_count, dtype=jnp.int32)).astype(
        jnp.bfloat16
    )
    left_dense = jnp.einsum(
        "nkab,nkj->najb", all_values, left_picker, preferred_element_type=jnp.float32
    )
    left_dense = left_dense.astype(jnp.bfloat16).reshape(rows_block * TILE, inner_count * TILE)
    expanded = jnp.dot(left_dense, all_panels, preferred_element_type=jnp.float32)
    squares = expanded * expanded
    column_part = jnp.sum(squares, axis=0)
    column_total = over_copies(column_part, ROW)
    factor = tile_count * TILE / (column_total + 1e-06)
    return (squares * factor).astype(jnp.bfloat16)


def solution(mesh):
    split = Mesh(
        mesh.devices.reshape(4, 2, 2, mesh.shape["col"]), ("row_0", "row_1", "row_2", "col")
    )
    in_specs = (P(ROW_COL, None, None, None, None), P(ROW_COL, None, None), P(), P())
    out_specs = P(ROW, "col")
    return jax.shard_map(
        per_device, mesh=split, in_specs=in_specs, out_specs=out_specs, check_vma=False
    )
```

profile of v0, /device:TPU:1, one launch (start us, length us, event | category | flops | bytes accessed | tf_op | source)
XLA Modules:
  0.0 567.8 jit_solution(13753688839111758612)
XLA Ops:
  6.5 3.2 copy.88
  9.7 6.5 %all-to-all-start = ((bf16[2,8,4,128,128]{4,3,2,0,1:T(8,128)(2,1)}), bf16[2,8,4,128,128]{4,3,2,0,1:T(8,128)(2,1)S(1)}, u32[]{:S(2)}, u32[]{:S(2)}) async-start(bf16[2,8,4,128,128]{4,3,2,0,1:T(8,128)(2,1)} %copy.88), calls=%async_computation | async-start | bytes 4194304 | tf_op jit(solution)/shard_map/all_to_all | solution.py:79
  16.2 0.7 gather_fusion.1
  16.9 3.2 sort.49
  20.1 1.3 sort.48
  21.5 25.3 %all-to-all-done = bf16[2,8,4,128,128]{4,3,2,0,1:T(8,128)(2,1)S(1)} async-done(((bf16[2,8,4,128,128]{4,3,2,0,1:T(8,128)(2,1)}), bf16[2,8,4,128,128]{4,3,2,0,1:T(8,128)(2,1)S(1)}, u32[]{:S(2)}, u32[]{:S(2)}) %all-to-all-start) | async-done | bytes 2097184 | tf_op jit(solution)/shard_map/all_to_all | solution.py:79
  46.8 2.1 gather_fusion.2
  48.9 1.7 copy.89
  50.7 6.6 %all_to_all.31 = bf16[8,2,1,4,128,128]{5,4,3,0,2,1:T(8,128)(2,1)S(1)} all-to-all(bf16[8,2,1,4,128,128]{5,4,3,0,2,1:T(8,128)(2,1)S(1)} %copy.89), channel_id=1, replica_groups=mesh['row_0'=4,'row_1'=2,'row_2'=2,'col'=8] {'row_2'}, dimensions={1} | all-to-all | bytes 4194304 | tf_op jit(solution)/shard_map/all_to_all | solution.py:30
  57.3 1.5 copy.90
  58.7 7.2 %all-to-all-start.2 = ((bf16[8,2,1,4,128,128]{5,4,3,1,2,0:T(8,128)(2,1)}), bf16[8,2,1,4,128,128]{5,4,3,1,2,0:T(8,128)(2,1)S(1)}, u32[]{:S(2)}, u32[]{:S(2)}) async-start(bf16[8,2,1,4,128,128]{5,4,3,1,2,0:T(8,128)(2,1)} %copy.90), calls=%async_computation.2 | async-start | bytes 4194304 | tf_op jit(solution)/shard_map/all_to_all | solution.py:30
  69.1 0.7 gather_fusion.3
  69.8 1.3 sort.50
  71.1 25.7 %all-to-all-done.2 = bf16[8,2,1,4,128,128]{5,4,3,1,2,0:T(8,128)(2,1)S(1)} async-done(((bf16[8,2,1,4,128,128]{5,4,3,1,2,0:T(8,128)(2,1)}), bf16[8,2,1,4,128,128]{5,4,3,1,2,0:T(8,128)(2,1)S(1)}, u32[]{:S(2)}, u32[]{:S(2)}) %all-to-all-start.2) | async-done | bytes 2097184 | tf_op jit(solution)/shard_map/all_to_all | solution.py:30
  96.8 2.1 gather_fusion.4
  99.0 7.6 %broadcast_select_fusion.3 = (bf16[16,4,128,128]{3,1,2,0:T(4,128)(2,1)}, bf16[16,4,128,128]{3,1,2,0:T(4,128)(2,1)}, bf16[16,4,128,128]{3,1,2,0:T(4,128)(2,1)}, bf16[16,4,128,128]{3,1,2,0:T(4,128)(2,1)}) fusion(pred[]{:T(512)S(6)} %eq.60, bf16[16,4,128,128]{3,2,1,0:T(8,128)(2,1)} %gather_fusion.4, pred[]{:T(512)S(6)} %eq.63, pred[]{:T(512)S(6)} %eq.67, ...), kind=kLoop, calls=%fused_computation.21 | loop fusion | flops 4194304 | bytes 10485764 | tf_op jit(solution)/shard_map/jit(_where)/select_n | solution.py:42
  106.7 0.7 all-reduce.7.cloned.1.call-update
  108.7 1.4 scatter_custom_fusion
  110.1 301.1 %all_gather.3 = s32[256,8,4]{1,2,0:T(4,128)S(1)} all-gather(s32[2,8,4]{1,2,0:T(4,128)S(1)} %copy-done.3), channel_id=1, replica_groups=mesh['row_0'=4,'row_1'=2,'row_2'=2,'col'=8] {'row_0','row_1','row_2','col'}, dimensions={0}, use_global_device_ids=true | all-gather | bytes 33024 | tf_op jit(solution)/shard_map/all_gather | solution.py:70
  411.2 1.0 gather_fusion
  413.2 7.1 %convert_bitcast_fusion = bf16[16,128,12,128]{3,2,1,0:T(8,128)(2,1)} fusion(bf16[16,4,128,128]{3,1,2,0:T(4,128)(2,1)} %get-tuple-element.23, s32[16,4]{1,0:T(8,128)S(1)} %copy.100), kind=kOutput, calls=%fused_computation.13 | convolution fusion | flops 28312320 | bytes 8388864 | tf_op jit(solution)/shard_map/nkab,nkj->najb/dot_general | solution.py:57
  420.4 12.2 %copy.102 = bf16[16,128,12,128]{1,3,2,0:T(8,128)(2,1)} copy(bf16[16,128,12,128]{3,2,1,0:T(8,128)(2,1)} %convert_bitcast_fusion) | data formatting | bytes 12582912 | tf_op jit(solution)/shard_map/convert_element_type | solution.py:58
  432.6 6.4 %convert_bitcast_fusion.1 = bf16[16,128,12,128]{3,2,1,0:T(8,128)(2,1)} fusion(bf16[16,4,128,128]{3,1,2,0:T(4,128)(2,1)S(1)} %copy-done.1, s32[16,4]{1,0:T(8,128)S(1)} %copy.96), kind=kOutput, calls=%fused_computation.14 | convolution fusion | flops 28312320 | bytes 8388864 | tf_op jit(solution)/shard_map/nkab,nkj->najb/dot_general | solution.py:57
  439.0 12.0 %copy.98 = bf16[16,128,12,128]{1,3,2,0:T(8,128)(2,1)} copy(bf16[16,128,12,128]{3,2,1,0:T(8,128)(2,1)} %convert_bitcast_fusion.1) | data formatting | bytes 12582912 | tf_op jit(solution)/shard_map/convert_element_type | solution.py:58
  451.0 10.5 %pad_maximum_fusion = bf16[32,128,1536]{1,2,0:T(8,128)(2,1)} fusion(bf16[16,128,1536]{1,2,0:T(8,128)(2,1)} %bitcast.70, bf16[16,128,1536]{1,2,0:T(8,128)(2,1)} %bitcast.71), kind=kLoop, calls=%fused_computation.9 | loop fusion | flops 6291456 | bytes 25165824 | tf_op jit(solution)/shard_map/concatenate | solution.py:110
  461.5 16.6 %copy.103 = bf16[32,128,1536]{2,1,0:T(8,128)(2,1)} copy(bf16[32,128,1536]{1,2,0:T(8,128)(2,1)} %pad_maximum_fusion) | data formatting | bytes 25165824 | tf_op jit(solution)/shard_map/concatenate | solution.py:110
  478.1 4.0 broadcast_multiply_fusion
  482.1 2.3 broadcast_multiply_fusion.1
  484.4 9.9 %convolution_convert_fusion = bf16[16,32,128,128]{3,1,2,0:T(8,128)(2,1)} fusion(bf16[16,4,128,128]{3,1,2,0:T(4,128)(2,1)} %broadcast_multiply_fusion, bf16[16,4,128,128]{3,1,2,0:T(4,128)(2,1)} %broadcast_multiply_fusion.1, s32[16,8]{1,0:T(8,128)S(1)} %copy.87), kind=kOutput, calls=%fused_computation.12 | convolution fusion | flops 150999040 | bytes 20972032 | tf_op jit(solution)/shard_map/nkab,nkj->najb/dot_general | solution.py:115
  494.3 31.4 %multiply_reduce_fusion = (f32[1536]{0:T(1024)S(1)}, f32[2048,1536]{1,0:T(8,128)}) fusion(bf16[4096,1536]{1,0:T(8,128)(2,1)S(1)} %bitcast.74, bf16[256,8,32,128]{3,2,1,0:T(8,128)(2,1)} %bitcast.69), kind=kOutput, calls=%fused_computation.11 | convolution fusion | flops 25776093184 | bytes 41949184 | tf_op jit(solution)/shard_map/dot_general | solution.py:119
  525.8 26.1 %all_to_all.32 = f32[16,1,1536]{2,1,0:T(1,128)S(1)} all-to-all(f32[16,1,1536]{2,1,0:T(1,128)S(1)} %broadcast_in_dim.48), channel_id=1, replica_groups=mesh['row_0'=4,'row_1'=2,'row_2'=2,'col'=8] {'row_0','row_1','row_2'}, dimensions={0} | all-to-all | bytes 196608 | tf_op jit(solution)/shard_map/all_to_all | solution.py:47
  551.9 9.0 %multiply_convert_fusion = bf16[2048,1536]{1,0:T(8,128)(2,1)} fusion(f32[2048,1536]{1,0:T(8,128)} %get-tuple-element.40, f32[1536]{0:T(1024)S(1)} %add_divide_fusion), kind=kLoop, calls=%fused_computation.10 | loop fusion | flops 9437184 | bytes 18880512 | tf_op jit(solution)/shard_map/convert_element_type | solution.py:124
  (57 shorter events, 2.0 us)
Async XLA Ops:
  9.7 6.5 %copy-start = (s32[256]{0:T(256)S(1)}, s32[256]{0:T(256)}, u32[]{:S(2)}) copy-start(s32[256]{0:T(256)} %param.8) | copy-start | bytes 3076
  9.7 37.1 %all-to-all-start = ((bf16[2,8,4,128,128]{4,3,2,0,1:T(8,128)(2,1)}), bf16[2,8,4,128,128]{4,3,2,0,1:T(8,128)(2,1)S(1)}, u32[]{:S(2)}, u32[]{:S(2)}) async-start(bf16[2,8,4,128,128]{4,3,2,0,1:T(8,128)(2,1)} %copy.88), calls=%async_computation | async-start | bytes 4194304 | tf_op jit(solution)/shard_map/all_to_all | solution.py:79
  58.7 7.2 %copy-start.4 = (s32[2]{0:T(128)S(1)}, s32[2]{0:T(128)}, u32[]{:S(2)}) copy-start(s32[2]{0:T(128)} %param.9) | copy-start | bytes 28
  58.7 38.1 %all-to-all-start.2 = ((bf16[8,2,1,4,128,128]{5,4,3,1,2,0:T(8,128)(2,1)}), bf16[8,2,1,4,128,128]{5,4,3,1,2,0:T(8,128)(2,1)S(1)}, u32[]{:S(2)}, u32[]{:S(2)}) async-start(bf16[8,2,1,4,128,128]{5,4,3,1,2,0:T(8,128)(2,1)} %copy.90), calls=%async_computation.2 | async-start | bytes 4194304 | tf_op jit(solution)/shard_map/all_to_all | solution.py:30
  65.9 347.3 %all-reduce.5.cloned.1.call-start = ((), (), s32[]{:S(2)}) async-start(), calls=%async_computation.4 | async-start | bytes 8388608 | tf_op jit(solution)/shard_map/psum | solution.py:42
  106.6 371.5 %all-reduce.7.cloned.1.call-start = ((), (), s32[]{:S(2)}) async-start(), calls=%async_computation.5 | async-start | bytes 8388608 | tf_op jit(solution)/shard_map/psum | solution.py:42
  106.7 3.4 copy-start.3
  420.3 12.2 %copy-start.1 = (bf16[16,4,128,128]{3,1,2,0:T(4,128)(2,1)S(1)}, bf16[16,4,128,128]{3,1,2,0:T(4,128)(2,1)}, u32[]{:S(2)}) copy-start(bf16[16,4,128,128]{3,1,2,0:T(4,128)(2,1)} %get-tuple-element.24) | copy-start | bytes 6291460
  478.1 4.0 copy-start.2
  482.1 12.2 %slice-start = ((s8[12582912]{0:T(1024)(128)(4,1)}), s8[4194304]{0:T(1024)(128)(4,1)S(1)}, s32[]{:S(2)}) async-start(s8[12582912]{0:T(1024)(128)(4,1)} %bitcast.72), calls=%async_computation.6 | async-start | bytes 8388608
  484.4 9.9 %slice-start.1 = ((s8[12582912]{0:T(1024)(128)(4,1)}), s8[4194304]{0:T(1024)(128)(4,1)S(1)}, s32[]{:S(2)}) async-start(s8[12582912]{0:T(1024)(128)(4,1)} %bitcast.72), calls=%async_computation.7 | async-start | bytes 8388608
  484.4 9.9 %slice-start.2 = ((s8[12582912]{0:T(1024)(128)(4,1)}), s8[4194304]{0:T(1024)(128)(4,1)S(1)}, s32[]{:S(2)}) async-start(s8[12582912]{0:T(1024)(128)(4,1)} %bitcast.72), calls=%async_computation.8 | async-start | bytes 8388608
Sparse Core Ops, SparseCore 0:
  106.7 147.2 all-reduce.4
  256.6 187.8 all-reduce.6
where the time goes:
time: 569 us; the launch traced here: 568 us
  blocking collectives  334 us (59%)
  local copies, waits for them, and re-layouts  56.7 us (10%)
  matrix products  54.8 us (10%)
  waiting for transfers between devices  51.8 us (9%)
  other arithmetic  39.6 us (7%)
  between operations  17.4 us (3%)
  starting transfers between devices  13.7 us (2%)
    all_gather x1, blocking collectives, per_device(): every_columns = lax.all_gather(tile_columns, ROW_COL, axis=0, tiled=True)  301 us
    dot_general x1, matrix products, per_device(): jnp.dot(left_dense, all_panels, preferred_element_type=jnp.float32)  31.4 us
    all_to_all x1, blocking collectives, copy_for_each(): lax.all_to_all(jnp.broadcast_to(x[None], (peers, *x.shape)), axis, 0, 0,...  26.1 us
    all_to_all x1, waiting for transfers between devices, moved_by_axis(): out = lax.all_to_all(out, axes[k], k, k, tiled=True)  25.7 us
    all_to_all x1, waiting for transfers between devices, per_device(): lax.all_to_all(tile_values, 'col', split_axis=1, concat_axis=0, tiled=True)  25.3 us
    convert_element_type x2, local copies, waits for them, and re-layouts, densify(): spread.astype(jnp.bfloat16).reshape(values_in.shape[0], TILE, SLAB * TILE)  24.2 us
    concatenate x1, local copies, waits for them, and re-layouts, per_device(): jnp.concatenate(panels, axis=0)  16.6 us
    dot_general x2, matrix products, densify(): jnp.einsum('nkab,nkj->najb', values_in, picker, preferred_element_type=jn...  13.5 us
  transfers between devices with their start and end apart: 4, of which 2 were waited for; matrix products, arithmetic and copies ran while one was open for 13% of the time, Pallas kernels for 0%

commit v1 on v0

--- a/solution.py
+++ b/solution.py
@@ -67,7 +67,12 @@
     rows_block = tile_values.shape[0] * n_col
     cols_block = tile_values.shape[0] * n_row
     first_col = col_id * cols_block
-    every_columns = lax.all_gather(tile_columns, ROW_COL, axis=0, tiled=True)
+    every_columns = jnp.concatenate(
+        jax.lax.all_to_all(
+            jnp.stack(jax.lax.axis_size(ROW_COL) * [tile_columns], axis=0), ROW_COL, 0, 0
+        ),
+        0,
+    )
     every_tile = jnp.arange(tile_count, dtype=jnp.int32)
     inverse = jnp.zeros((tile_count,), jnp.int32).at[owner_map].set(every_tile)
     grid_columns = every_columns[inverse]

time: 569 us -> 525 us (0.923)
  blocking collectives: 334 us -> 21.2 us
  waiting for transfers between devices: 51.8 us -> 314 us
    all_gather x1 -> x0, blocking collectives: 301 us -> none  [per_device(): every_columns = lax.all_gather(tile_columns, ROW_COL, axis=0, tiled=True)]
    psum x2, waiting for transfers between devices: 0.01 us -> 250 us  [broadcast(): return lax.psum(jnp.where(mine, x, jnp.zeros_like(x)), axis)]
    all_to_all x0 -> x1, waiting for transfers between devices: none -> 12.2 us  [per_device(): jax.lax.all_to_all(jnp.stack(jax.lax.axis_size(ROW_COL) * [tile_columns],...]
    all_to_all x1, blocking collectives: 26.1 us -> 14.6 us  [copy_for_each(): lax.all_to_all(jnp.broadcast_to(x[None], (peers, *x.shape)), axis, 0, 0,...]
  transfers between devices with their start and end apart: 4 -> 5, of which waited for: 2 -> 5; matrix products, arithmetic and copies ran while one was open for 13% -> 15% of each run, Pallas kernels for 0% -> 0%
where the time goes in v1:
time: 525 us; the launch traced here: 524 us
  waiting for transfers between devices  314 us (60%)
  local copies, waits for them, and re-layouts  57.8 us (11%)
  matrix products  54.8 us (10%)
  other arithmetic  39.7 us (8%)
  blocking collectives  21.2 us (4%)
  starting transfers between devices  18.6 us (4%)
  between operations  17.4 us (3%)
    psum x2, waiting for transfers between devices, broadcast(): return lax.psum(jnp.where(mine, x, jnp.zeros_like(x)), axis)  250 us
    dot_general x1, matrix products, per_device(): jnp.dot(left_dense, all_panels, preferred_element_type=jnp.float32)  31.4 us
    all_to_all x1, waiting for transfers between devices, moved_by_axis(): out = lax.all_to_all(out, axes[k], k, k, tiled=True)  25.7 us
    all_to_all x1, waiting for transfers between devices, per_device(): lax.all_to_all(tile_values, 'col', split_axis=1, concat_axis=0, tiled=True)  25.3 us
    convert_element_type x2, local copies, waits for them, and re-layouts, densify(): spread.astype(jnp.bfloat16).reshape(values_in.shape[0], TILE, SLAB * TILE)  24.2 us
    concatenate x1, local copies, waits for them, and re-layouts, per_device(): jnp.concatenate(panels, axis=0)  16.7 us
    all_to_all x1, blocking collectives, copy_for_each(): lax.all_to_all(jnp.broadcast_to(x[None], (peers, *x.shape)), axis, 0, 0,...  14.6 us
    dot_general x2, matrix products, densify(): jnp.einsum('nkab,nkj->najb', values_in, picker, preferred_element_type=jn...  13.5 us
  transfers between devices with their start and end apart: 5, of which 5 were waited for; matrix products, arithmetic and copies ran while one was open for 15% of the time, Pallas kernels for 0%

profile of v1, /device:TPU:1, one launch (start us, length us, event | category | flops | bytes accessed | tf_op | source)
XLA Modules:
  0.0 523.6 jit_solution(7952647315136389395)
XLA Ops:
  6.5 3.2 copy.85
  9.7 6.5 %all-to-all-start.1 = ((bf16[2,8,4,128,128]{4,3,2,0,1:T(8,128)(2,1)}), bf16[2,8,4,128,128]{4,3,2,0,1:T(8,128)(2,1)S(1)}, u32[]{:S(2)}, u32[]{:S(2)}) async-start(bf16[2,8,4,128,128]{4,3,2,0,1:T(8,128)(2,1)} %copy.85), calls=%async_computation.1 | async-start | bytes 4194304 | tf_op jit(solution)/shard_map/all_to_all | solution.py:84
  16.9 3.2 sort.49
  20.1 1.3 sort.48
  21.5 25.3 %all-to-all-done.1 = bf16[2,8,4,128,128]{4,3,2,0,1:T(8,128)(2,1)S(1)} async-done(((bf16[2,8,4,128,128]{4,3,2,0,1:T(8,128)(2,1)}), bf16[2,8,4,128,128]{4,3,2,0,1:T(8,128)(2,1)S(1)}, u32[]{:S(2)}, u32[]{:S(2)}) %all-to-all-start.1) | async-done | bytes 2097184 | tf_op jit(solution)/shard_map/all_to_all | solution.py:84
  46.8 2.1 gather_fusion.2
  48.9 1.7 copy.86
  50.7 6.6 %all_to_all.36 = bf16[8,2,1,4,128,128]{5,4,3,0,2,1:T(8,128)(2,1)S(1)} all-to-all(bf16[8,2,1,4,128,128]{5,4,3,0,2,1:T(8,128)(2,1)S(1)} %copy.86), channel_id=1, replica_groups=mesh['row_0'=4,'row_1'=2,'row_2'=2,'col'=8] {'row_2'}, dimensions={1} | all-to-all | bytes 4194304 | tf_op jit(solution)/shard_map/all_to_all | solution.py:30
  57.3 1.5 copy.87
  58.7 7.2 %all-to-all-start.3 = ((bf16[8,2,1,4,128,128]{5,4,3,1,2,0:T(8,128)(2,1)}), bf16[8,2,1,4,128,128]{5,4,3,1,2,0:T(8,128)(2,1)S(1)}, u32[]{:S(2)}, u32[]{:S(2)}) async-start(bf16[8,2,1,4,128,128]{5,4,3,1,2,0:T(8,128)(2,1)} %copy.87), calls=%async_computation.3 | async-start | bytes 4194304 | tf_op jit(solution)/shard_map/all_to_all | solution.py:30
  69.8 1.3 sort.50
  71.1 25.7 %all-to-all-done.3 = bf16[8,2,1,4,128,128]{5,4,3,1,2,0:T(8,128)(2,1)S(1)} async-done(((bf16[8,2,1,4,128,128]{5,4,3,1,2,0:T(8,128)(2,1)}), bf16[8,2,1,4,128,128]{5,4,3,1,2,0:T(8,128)(2,1)S(1)}, u32[]{:S(2)}, u32[]{:S(2)}) %all-to-all-start.3) | async-done | bytes 2097184 | tf_op jit(solution)/shard_map/all_to_all | solution.py:30
  96.8 2.1 gather_fusion.4
  99.0 7.6 %broadcast_select_fusion.3 = (bf16[16,4,128,128]{3,1,2,0:T(4,128)(2,1)}, bf16[16,4,128,128]{3,1,2,0:T(4,128)(2,1)}, bf16[16,4,128,128]{3,1,2,0:T(4,128)(2,1)}, bf16[16,4,128,128]{3,1,2,0:T(4,128)(2,1)}) fusion(pred[]{:T(512)S(6)} %eq.60, bf16[16,4,128,128]{3,2,1,0:T(8,128)(2,1)} %gather_fusion.4, pred[]{:T(512)S(6)} %eq.63, pred[]{:T(512)S(6)} %eq.67, ...), kind=kLoop, calls=%fused_computation.21 | loop fusion | flops 4194304 | bytes 10485764 | tf_op jit(solution)/shard_map/jit(_where)/select_n | solution.py:42
  108.2 4.8 all-to-all-start
  113.1 1.6 scatter_custom_fusion
  116.0 12.2 %all-to-all-done = s32[128,2,8,4]{2,3,1,0:T(4,128)S(1)} async-done(((s32[128,2,8,4]{2,3,1,0:T(4,128)}), s32[128,2,8,4]{2,3,1,0:T(4,128)S(1)}, u32[]{:S(2)}, u32[]{:S(2)}) %all-to-all-start) | async-done | bytes 32800 | tf_op jit(solution)/shard_map/all_to_all | solution.py:71
  128.2 1.0 gather_fusion
  130.2 129.4 %all-reduce.5.cloned.1.call-done = (bf16[16,4,128,128]{3,1,2,0:T(4,128)(2,1)}, bf16[16,4,128,128]{3,1,2,0:T(4,128)(2,1)}) async-done(((bf16[16,4,128,128]{3,1,2,0:T(4,128)(2,1)}, bf16[16,4,128,128]{3,1,2,0:T(4,128)(2,1)}), (bf16[16,4,128,128]{3,1,2,0:T(4,128)(2,1)}, bf16[16,4,128,128]{3,1,2,0:T(4,128)(2,1)})) %all-reduce.5.cloned.1.call-update) | async-done | bytes 4194320 | tf_op jit(solution)/shard_map/psum | solution.py:42
  259.7 7.1 %convert_bitcast_fusion = bf16[16,128,12,128]{3,2,1,0:T(8,128)(2,1)} fusion(bf16[16,4,128,128]{3,1,2,0:T(4,128)(2,1)} %get-tuple-element.23, s32[16,4]{1,0:T(8,128)S(1)} %copy.97), kind=kOutput, calls=%fused_computation.13 | convolution fusion | flops 28312320 | bytes 8388864 | tf_op jit(solution)/shard_map/nkab,nkj->najb/dot_general | solution.py:57
  266.8 12.2 %copy.99 = bf16[16,128,12,128]{1,3,2,0:T(8,128)(2,1)} copy(bf16[16,128,12,128]{3,2,1,0:T(8,128)(2,1)} %convert_bitcast_fusion) | data formatting | bytes 12582912 | tf_op jit(solution)/shard_map/convert_element_type | solution.py:58
  279.0 6.4 %convert_bitcast_fusion.1 = bf16[16,128,12,128]{3,2,1,0:T(8,128)(2,1)} fusion(bf16[16,4,128,128]{3,1,2,0:T(4,128)(2,1)S(1)} %copy-done.1, s32[16,4]{1,0:T(8,128)S(1)} %copy.93), kind=kOutput, calls=%fused_computation.14 | convolution fusion | flops 28312320 | bytes 8388864 | tf_op jit(solution)/shard_map/nkab,nkj->najb/dot_general | solution.py:57
  285.4 12.0 %copy.95 = bf16[16,128,12,128]{1,3,2,0:T(8,128)(2,1)} copy(bf16[16,128,12,128]{3,2,1,0:T(8,128)(2,1)} %convert_bitcast_fusion.1) | data formatting | bytes 12582912 | tf_op jit(solution)/shard_map/convert_element_type | solution.py:58
  297.4 10.5 %pad_maximum_fusion = bf16[32,128,1536]{1,2,0:T(8,128)(2,1)} fusion(bf16[16,128,1536]{1,2,0:T(8,128)(2,1)} %bitcast.71, bf16[16,128,1536]{1,2,0:T(8,128)(2,1)} %bitcast.72), kind=kLoop, calls=%fused_computation.9 | loop fusion | flops 6291456 | bytes 25165824 | tf_op jit(solution)/shard_map/concatenate | solution.py:115
  307.9 16.7 %copy.100 = bf16[32,128,1536]{2,1,0:T(8,128)(2,1)} copy(bf16[32,128,1536]{1,2,0:T(8,128)(2,1)} %pad_maximum_fusion) | data formatting | bytes 25165824 | tf_op jit(solution)/shard_map/concatenate | solution.py:115
  324.6 120.8 %all-reduce.7.cloned.1.call-done = (bf16[16,4,128,128]{3,1,2,0:T(4,128)(2,1)}, bf16[16,4,128,128]{3,1,2,0:T(4,128)(2,1)}) async-done(((bf16[16,4,128,128]{3,1,2,0:T(4,128)(2,1)}, bf16[16,4,128,128]{3,1,2,0:T(4,128)(2,1)}), (bf16[16,4,128,128]{3,1,2,0:T(4,128)(2,1)}, bf16[16,4,128,128]{3,1,2,0:T(4,128)(2,1)})) %all-reduce.7.cloned.1.call-update) | async-done | bytes 4194320 | tf_op jit(solution)/shard_map/psum | solution.py:42
  445.3 4.0 broadcast_multiply_fusion
  449.4 2.3 broadcast_multiply_fusion.1
  451.7 9.8 %convolution_convert_fusion = bf16[16,32,128,128]{3,1,2,0:T(8,128)(2,1)} fusion(bf16[16,4,128,128]{3,1,2,0:T(4,128)(2,1)} %broadcast_multiply_fusion, bf16[16,4,128,128]{3,1,2,0:T(4,128)(2,1)} %broadcast_multiply_fusion.1, s32[16,8]{1,0:T(8,128)S(1)} %copy.84), kind=kOutput, calls=%fused_computation.12 | convolution fusion | flops 150999040 | bytes 20972032 | tf_op jit(solution)/shard_map/nkab,nkj->najb/dot_general | solution.py:120
  461.6 31.4 %multiply_reduce_fusion = (f32[1536]{0:T(1024)S(1)}, f32[2048,1536]{1,0:T(8,128)}) fusion(bf16[4096,1536]{1,0:T(8,128)(2,1)S(1)} %bitcast.75, bf16[256,8,32,128]{3,2,1,0:T(8,128)(2,1)} %bitcast.70), kind=kOutput, calls=%fused_computation.11 | convolution fusion | flops 25776093184 | bytes 41949184 | tf_op jit(solution)/shard_map/dot_general | solution.py:124
  493.0 14.6 %all_to_all.37 = f32[16,1,1536]{2,1,0:T(1,128)S(1)} all-to-all(f32[16,1,1536]{2,1,0:T(1,128)S(1)} %broadcast_in_dim.48), channel_id=1, replica_groups=mesh['row_0'=4,'row_1'=2,'row_2'=2,'col'=8] {'row_0','row_1','row_2'}, dimensions={0} | all-to-all | bytes 196608 | tf_op jit(solution)/shard_map/all_to_all | solution.py:47
  507.7 9.0 %multiply_convert_fusion = bf16[2048,1536]{1,0:T(8,128)(2,1)} fusion(f32[2048,1536]{1,0:T(8,128)} %get-tuple-element.40, f32[1536]{0:T(1024)S(1)} %add_divide_fusion), kind=kLoop, calls=%fused_computation.10 | loop fusion | flops 9437184 | bytes 18880512 | tf_op jit(solution)/shard_map/convert_element_type | solution.py:129
  (59 shorter events, 4.9 us)
Async XLA Ops:
  9.7 6.5 %copy-start = (s32[256]{0:T(256)S(1)}, s32[256]{0:T(256)}, u32[]{:S(2)}) copy-start(s32[256]{0:T(256)} %param.8) | copy-start | bytes 3076
  9.7 37.1 %all-to-all-start.1 = ((bf16[2,8,4,128,128]{4,3,2,0,1:T(8,128)(2,1)}), bf16[2,8,4,128,128]{4,3,2,0,1:T(8,128)(2,1)S(1)}, u32[]{:S(2)}, u32[]{:S(2)}) async-start(bf16[2,8,4,128,128]{4,3,2,0,1:T(8,128)(2,1)} %copy.85), calls=%async_computation.1 | async-start | bytes 4194304 | tf_op jit(solution)/shard_map/all_to_all | solution.py:84
  58.7 7.2 %copy-start.4 = (s32[2]{0:T(128)S(1)}, s32[2]{0:T(128)}, u32[]{:S(2)}) copy-start(s32[2]{0:T(128)} %param.9) | copy-start | bytes 28
  58.7 38.1 %all-to-all-start.3 = ((bf16[8,2,1,4,128,128]{5,4,3,1,2,0:T(8,128)(2,1)}), bf16[8,2,1,4,128,128]{5,4,3,1,2,0:T(8,128)(2,1)S(1)}, u32[]{:S(2)}, u32[]{:S(2)}) async-start(bf16[8,2,1,4,128,128]{5,4,3,1,2,0:T(8,128)(2,1)} %copy.87), calls=%async_computation.3 | async-start | bytes 4194304 | tf_op jit(solution)/shard_map/all_to_all | solution.py:30
  65.9 193.7 %all-reduce.5.cloned.1.call-start = ((), (), s32[]{:S(2)}) async-start(), calls=%async_computation.5 | async-start | bytes 8388608 | tf_op jit(solution)/shard_map/psum | solution.py:42
  106.6 338.7 %all-reduce.7.cloned.1.call-start = ((), (), s32[]{:S(2)}) async-start(), calls=%async_computation.6 | async-start | bytes 8388608 | tf_op jit(solution)/shard_map/psum | solution.py:42
  106.7 0.7 copy-start.3
  108.2 19.9 %all-to-all-start = ((s32[128,2,8,4]{2,3,1,0:T(4,128)}), s32[128,2,8,4]{2,3,1,0:T(4,128)S(1)}, u32[]{:S(2)}, u32[]{:S(2)}) async-start(s32[128,2,8,4]{2,3,1,0:T(4,128)} %stack.2), calls=%async_computation | async-start | bytes 1048576 | tf_op jit(solution)/shard_map/all_to_all | solution.py:71
  266.8 12.2 %copy-start.1 = (bf16[16,4,128,128]{3,1,2,0:T(4,128)(2,1)S(1)}, bf16[16,4,128,128]{3,1,2,0:T(4,128)(2,1)}, u32[]{:S(2)}) copy-start(bf16[16,4,128,128]{3,1,2,0:T(4,128)(2,1)} %get-tuple-element.24) | copy-start | bytes 6291460
  445.3 4.0 copy-start.2
  449.4 12.2 %slice-start = ((s8[12582912]{0:T(1024)(128)(4,1)}), s8[4194304]{0:T(1024)(128)(4,1)S(1)}, s32[]{:S(2)}) async-start(s8[12582912]{0:T(1024)(128)(4,1)} %bitcast.73), calls=%async_computation.7 | async-start | bytes 8388608
  451.7 9.9 %slice-start.1 = ((s8[12582912]{0:T(1024)(128)(4,1)}), s8[4194304]{0:T(1024)(128)(4,1)S(1)}, s32[]{:S(2)}) async-start(s8[12582912]{0:T(1024)(128)(4,1)} %bitcast.73), calls=%async_computation.8 | async-start | bytes 8388608
  451.7 9.9 %slice-start.2 = ((s8[12582912]{0:T(1024)(128)(4,1)}), s8[4194304]{0:T(1024)(128)(4,1)S(1)}, s32[]{:S(2)}) async-start(s8[12582912]{0:T(1024)(128)(4,1)} %bitcast.73), calls=%async_computation.9 | async-start | bytes 8388608
Sparse Core Ops, SparseCore 0:
  106.7 152.8 all-reduce.4
  262.2 183.0 all-reduce.6
